TPU v7x, 32 devices: a whole 2x2x4 slice. The times are simulated.
32 devices in a mesh: expert: 4 (over y, x), shard: 8 (over z, core).
Axes of the slice: x: 2, y: 2, z: 4, core: 2. Of those that a mesh axis runs over, the one named last changes fastest.
Arguments:
- tokens: bfloat16 [256, 4096], P(('expert', 'shard')), may hold values from -6 to 6
- cotangent: bfloat16 [256, 4096], P(('expert', 'shard')), may hold values from -6 to 6
- expert_ids: int32 [256, 2], P(('expert', 'shard')), may hold values from 0 to 3, as said below
- slot_ids: int32 [256, 2], P(('expert', 'shard')), may hold values from 0 to 3, as said below
- route_weight: float32 [256, 2], P(('expert', 'shard')), may hold values from 0.1 to 1
- w_gate: bfloat16 [4, 4096, 7168], P('expert', 'shard'), may hold values from -0.09375 to 0.09375
- w_up: bfloat16 [4, 4096, 7168], P('expert', 'shard'), may hold values from -0.09375 to 0.09375
- w_down: bfloat16 [4, 4096, 7168], P('expert', 'shard'), may hold values from -0.0625 to 0.0625
Outputs:
- layer_out: bfloat16 [256, 4096], P(('expert', 'shard'))
- d_tokens: bfloat16 [256, 4096], P(('expert', 'shard'))
- grad_gate: bfloat16 [4, 4096, 7168], P('expert', 'shard')
- grad_up: bfloat16 [4, 4096, 7168], P('expert', 'shard')
- grad_down: bfloat16 [4, 4096, 7168], P('expert', 'shard')
Inputs may be any that keep to these rules, and one draw needn't show every extreme that they name: `expert_ids`: A token's two ids differ. Among the 8 tokens of one block no expert is named more than 4 times, and in every draw, for each index along shard, one expert is named exactly 4 times in each of the 4 blocks that share that index. Assignment k of a token takes slot slot_ids[., k] of the expert expert_ids[., k]; the assignments of one block to one expert have distinct slots.
All inputs are finite; a program needn't handle non-finite values.
Results may differ from a plain program's by a relative error of at most 0.019.
Values may be sent and summed in bfloat16 or wider, within the bound.
A program may use at most 128 MiB of HBM per device.

v0:
```python
import jax
import jax.numpy as jnp
from jax import lax
from jax.sharding import PartitionSpec as P

CAP = 4
BOTH = ("expert", "shard")


def per_device(tokens, cotangent, expert_ids, slot_ids, route_weight, w_gate, w_up, w_down):
    experts = lax.axis_size("expert")
    shards = lax.axis_size("shard")
    slots_all = experts * CAP
    rows = experts * shards * CAP
    width = tokens.shape[1]
    part = width // shards
    slot_index = expert_ids * CAP + slot_ids
    columns = jnp.arange(slots_all, dtype=jnp.int32)
    slot_match = (slot_index[:, :, None] == columns[None, None, :]).astype(jnp.float32)
    dispatch = jnp.sum(slot_match, axis=1).astype(jnp.bfloat16)
    combine = jnp.sum(slot_match * route_weight[:, :, None], axis=1)
    x_slots = jnp.einsum("tc,td->cd", dispatch, tokens, preferred_element_type=jnp.float32).astype(
        jnp.bfloat16
    )
    d_slots = jnp.dot(
        combine.T, cotangent.astype(jnp.float32), precision=lax.Precision.HIGHEST
    ).astype(jnp.bfloat16)

    def send(slots):
        pieces = slots.reshape(experts, CAP, shards, part).transpose(0, 2, 1, 3)
        return pieces.reshape(experts * shards, CAP, part)

    arrived = lax.all_to_all(
        jnp.concatenate([send(x_slots), send(d_slots)], axis=1),
        BOTH, split_axis=0, concat_axis=0, tiled=True,
    )
    x_rows = arrived[:, :CAP].reshape(rows, part)
    d_rows = arrived[:, CAP:].reshape(rows, part)
    hidden_units = w_gate.shape[2]

    def partial(left, right):
        return jnp.dot(left, right, preferred_element_type=jnp.float32).astype(jnp.bfloat16)

    parts = jnp.concatenate(
        [partial(x_rows, w_gate[0]), partial(x_rows, w_up[0]), partial(d_rows, w_down[0])], axis=0
    )
    summed = lax.psum_scatter(parts, "shard", scatter_dimension=0, tiled=True)
    full = lax.all_gather(summed, "shard", axis=0, tiled=True).astype(jnp.float32)
    gate_value, up_value, d_hidden = full[:rows], full[rows : 2 * rows], full[2 * rows :]
    logistic = jax.nn.sigmoid(gate_value)
    activation = gate_value * logistic
    silu_slope = logistic * (1.0 + gate_value * (1.0 - logistic))
    hidden = (activation * up_value).astype(jnp.bfloat16)
    d_gate = (d_hidden * up_value * silu_slope).astype(jnp.bfloat16)
    d_up = (d_hidden * activation).astype(jnp.bfloat16)

    def back(left, right):
        return jnp.einsum("rf,df->rd", left, right, preferred_element_type=jnp.float32)

    expert_out = back(hidden, w_down[0]).astype(jnp.bfloat16)
    d_expert = (back(d_gate, w_gate[0]) + back(d_up, w_up[0])).astype(jnp.bfloat16)
    returned = lax.all_to_all(
        jnp.concatenate(
            [expert_out.reshape(-1, CAP, part), d_expert.reshape(-1, CAP, part)], axis=1
        ),
        BOTH, split_axis=0, concat_axis=0, tiled=True,
    )

    def take(pieces):
        return pieces.reshape(experts, shards, CAP, part).transpose(0, 2, 1, 3).reshape(slots_all, width)

    layer_out = jnp.dot(
        combine, take(returned[:, :CAP]).astype(jnp.float32), precision=lax.Precision.HIGHEST
    ).astype(jnp.bfloat16)
    d_tokens = jnp.dot(
        dispatch, take(returned[:, CAP:]), preferred_element_type=jnp.float32
    ).astype(jnp.bfloat16)

    def grad(left, right):
        return jnp.einsum("rd,rf->df", left, right, preferred_element_type=jnp.float32).astype(
            jnp.bfloat16
        )

    return (
        layer_out,
        d_tokens,
        grad(x_rows, d_gate)[None],
        grad(x_rows, d_up)[None],
        grad(d_rows, hidden)[None],
    )


def solution(mesh):
    tok = P(BOTH, None)
    wt = P("expert", "shard", None)
    return jax.shard_map(
        per_device,
        mesh=mesh,
        in_specs=(tok,) * 5 + (wt,) * 3,
        out_specs=(tok,) * 2 + (wt,) * 3,
        check_vma=False,
    )
```

profile of v0, /device:TPU:0, one launch (start us, length us, event | category | flops | bytes accessed | tf_op | source)
XLA Modules:
  0.0 211.0 jit_solution(10106898388113795848)
XLA Ops:
  7.2 0.0 reduce-scatter.2.cloned.1.call-start
  7.2 0.7 multiply_add_fusion
  7.9 0.8 convert_reduce_fusion
  8.7 0.2 convolution_convert_fusion.7
  9.0 1.2 convolution_convert_fusion.6
  10.2 0.2 copy.40
  10.4 17.1 %all_to_all.10 = bf16[32,8,512]{2,1,0:T(8,128)(2,1)S(1)} all-to-all(bf16[32,8,512]{2,1,0:T(8,128)(2,1)S(1)} %copy.40), channel_id=1, replica_groups=mesh['expert'=4,'shard'=8] {'expert','shard'}, dimensions={0} | all-to-all | bytes 524288 | tf_op jit(solution)/shard_map/all_to_all | solution.py:33
  27.5 0.1 fusion.25
  27.7 4.4 %convolution_convert_fusion.4 = bf16[128,7168]{1,0:T(8,128)(2,1)S(1)} fusion(bf16[128,512]{1,0:T(8,128)(2,1)S(1)} %reshape.52, bf16[1,512,7168]{2,1,0:T(8,128)(2,1)} %param.14), kind=kOutput, calls=%fused_computation.7 | convolution fusion | flops 940441600 | bytes 9306112 | tf_op jit(solution)/shard_map/dot_general | solution.py:42
  32.1 0.8 copy-done.2
  32.9 1.2 convolution_convert_fusion.5
  34.1 1.1 slice-done.1
  35.2 1.2 convolution_convert_fusion.3
  36.5 3.0 %pad_maximum_fusion = bf16[384,7168]{1,0:T(8,128)(2,1)} fusion(bf16[128,7168]{1,0:T(8,128)(2,1)S(1)} %convolution_convert_fusion.3, bf16[128,7168]{1,0:T(8,128)(2,1)S(1)} %convolution_convert_fusion.4, bf16[128,7168]{1,0:T(8,128)(2,1)S(1)} %convolution_convert_fusion.5), kind=kLoop, calls=%fused_computation.18 | loop fusion | flops 16515072 | bytes 11010048 | tf_op jit(solution)/shard_map/concatenate | solution.py:44
  39.4 0.0 reduce-scatter.2.cloned.1.call-update
  39.5 0.2 all-gather.2.cloned.1.call-start
  39.7 60.5 %reduce-scatter.2.cloned.1.call-done = bf16[48,7168]{1,0:T(8,128)(2,1)} async-done(((bf16[384,7168]{1,0:T(8,128)(2,1)}), bf16[48,7168]{1,0:T(8,128)(2,1)}) %reduce-scatter.2.cloned.1.call-update) | async-done | bytes 688144 | tf_op jit(solution)/shard_map/reduce_scatter | solution.py:47
  100.2 58.3 %all-gather.2.cloned.1.call-done = bf16[384,7168]{1,0:T(8,128)(2,1)} async-done(((bf16[48,7168]{1,0:T(8,128)(2,1)}), bf16[384,7168]{1,0:T(8,128)(2,1)}) %all-gather.2.cloned.1.call-update) | async-done | bytes 5505040 | tf_op jit(solution)/shard_map/all_gather | solution.py:48
  158.5 4.1 %convert_element_type.63 = f32[384,7168]{1,0:T(8,128)S(1)} convert(bf16[384,7168]{1,0:T(8,128)(2,1)} %all-gather.2.cloned.1.call-done) | non-fusion elementwise | flops 2752512 | bytes 16515072 | tf_op jit(solution)/shard_map/convert_element_type | solution.py:48
  162.5 2.9 %multiply_convert_fusion.2 = (bf16[128,7168]{1,0:T(8,128)(2,1)S(1)}, bf16[128,7168]{1,0:T(8,128)(2,1)}, bf16[128,7168]{1,0:T(8,128)(2,1)S(1)}) fusion(f32[384,7168]{1,0:T(8,128)S(1)} %convert_element_type.63), kind=kLoop, calls=%fused_computation.25 | loop fusion | flops 13762560 | bytes 16515072 | tf_op jit(solution)/shard_map/convert_element_type | solution.py:53
  165.4 1.2 copy-done.5
  166.7 2.6 %fusion.19 = bf16[128,512]{1,0:T(8,128)(2,1)S(1)} fusion(bf16[128,7168]{1,0:T(8,128)(2,1)S(1)} %get-tuple-element.7, bf16[1,512,7168]{2,1,0:T(8,128)(2,1)S(1)} %bitcast.80), kind=kOutput, calls=%fused_computation.30 | convolution fusion | flops 939589632 | bytes 9306112 | tf_op jit(solution)/shard_map/rf,df->rd/dot_general | solution.py:58
  169.3 5.8 %fusion.6 = f32[128,512]{1,0:T(8,128)S(1)} fusion(bf16[128,7168]{1,0:T(8,128)(2,1)S(1)} %get-tuple-element.9, bf16[1,512,7168]{2,1,0:T(8,128)(2,1)} %param.14), kind=kOutput, calls=%fused_computation.12 | convolution fusion | flops 939524096 | bytes 9437184 | tf_op jit(solution)/shard_map/rf,df->rd/dot_general | solution.py:58
  175.1 5.7 %fusion.16 = bf16[128,512]{1,0:T(8,128)(2,1)S(1)} fusion(f32[128,512]{1,0:T(8,128)S(1)} %fusion.6, bf16[128,7168]{1,0:T(8,128)(2,1)S(1)} %copy-done.3, bf16[1,512,7168]{2,1,0:T(8,128)(2,1)} %param.13), kind=kOutput, calls=%fused_computation.29 | convolution fusion | flops 939655168 | bytes 9568256 | tf_op jit(solution)/shard_map/rf,df->rd/dot_general | solution.py:58
  180.8 0.8 pad_maximum_fusion.2
  181.7 3.6 %all-to-all-start.1 = ((bf16[32,8,512]{2,1,0:T(8,128)(2,1)}), bf16[32,8,512]{2,1,0:T(8,128)(2,1)S(1)}, u32[]{:S(2)}, u32[]{:S(2)}) async-start(bf16[32,8,512]{2,1,0:T(8,128)(2,1)} %pad_maximum_fusion.2), calls=%async_computation.2 | async-start | bytes 524288 | tf_op jit(solution)/shard_map/all_to_all | solution.py:62
  185.2 6.8 %fusion.2 = bf16[1,512,7168]{2,1,0:T(8,128)(2,1)} fusion(bf16[128,512]{1,0:T(8,128)(2,1)S(1)} %reshape.53, bf16[128,7168]{1,0:T(8,128)(2,1)} %copy-done.5), kind=kOutput, calls=%fused_computation.5 | convolution fusion | flops 943194112 | bytes 9306112 | tf_op jit(solution)/shard_map/rd,rf->df/dot_general | solution.py:80
  192.0 5.1 %fusion = bf16[1,512,7168]{2,1,0:T(8,128)(2,1)} fusion(bf16[128,512]{1,0:T(8,128)(2,1)S(1)} %reshape.52, bf16[128,7168]{1,0:T(8,128)(2,1)S(1)} %copy-done.4), kind=kOutput, calls=%fused_computation.3 | convolution fusion | flops 943194112 | bytes 9306112 | tf_op jit(solution)/shard_map/rd,rf->df/dot_general | solution.py:80
  197.2 5.1 %fusion.1 = bf16[1,512,7168]{2,1,0:T(8,128)(2,1)} fusion(bf16[128,512]{1,0:T(8,128)(2,1)S(1)} %reshape.52, bf16[128,7168]{1,0:T(8,128)(2,1)S(1)} %get-tuple-element.9), kind=kOutput, calls=%fused_computation.4 | convolution fusion | flops 943194112 | bytes 9306112 | tf_op jit(solution)/shard_map/rd,rf->df/dot_general | solution.py:80
  202.3 0.1 fusion.24
  202.5 0.8 convolution_convert_fusion.8
  203.4 0.8 convolution_convert_fusion.9
  (35 shorter events, 0.5 us)
Async XLA Ops:
  7.2 1.5 copy-start
  7.2 93.0 %reduce-scatter.2.cloned.1.call-start = ((), (), s32[]{:S(2)}) async-start(), calls=%async_computation.3 | async-start | bytes 6193152 | tf_op jit(solution)/shard_map/reduce_scatter | solution.py:47
  27.7 5.2 %copy-start.2 = (bf16[1,512,7168]{2,1,0:T(8,128)(2,1)S(1)}, bf16[1,512,7168]{2,1,0:T(8,128)(2,1)}, u32[]{:S(2)}) copy-start(bf16[1,512,7168]{2,1,0:T(8,128)(2,1)} %param.13) | copy-start | bytes 22020100
  27.7 6.4 %slice-start = ((s8[7340032]{0:T(1024)(128)(4,1)}), s8[4194304]{0:T(1024)(128)(4,1)S(1)}, s32[]{:S(2)}) async-start(s8[7340032]{0:T(1024)(128)(4,1)} %bitcast.77), calls=%async_computation.5 | async-start | bytes 8388608
  32.9 2.3 %slice-start.1 = ((s8[7340032]{0:T(1024)(128)(4,1)}), s8[3145728]{0:T(1024)(128)(4,1)S(1)}, s32[]{:S(2)}) async-start(s8[7340032]{0:T(1024)(128)(4,1)} %bitcast.77), calls=%async_computation.6 | async-start | bytes 6291456
  39.5 119.0 %all-gather.2.cloned.1.call-start = ((), (), s32[]{:S(2)}) async-start(), calls=%async_computation.4 | async-start | bytes 6193152 | tf_op jit(solution)/shard_map/all_gather | solution.py:48
  158.5 8.2 %slice-start.2 = ((s8[7340032]{0:T(1024)(128)(4,1)}), s8[3145728]{0:T(1024)(128)(4,1)S(1)}, s32[]{:S(2)}) async-start(s8[7340032]{0:T(1024)(128)(4,1)} %bitcast.79), calls=%async_computation.7 | async-start | bytes 6291456
  162.5 4.1 %slice-start.3 = ((s8[7340032]{0:T(1024)(128)(4,1)}), s8[4194304]{0:T(1024)(128)(4,1)S(1)}, s32[]{:S(2)}) async-start(s8[7340032]{0:T(1024)(128)(4,1)} %bitcast.79), calls=%async_computation.8 | async-start | bytes 8388608
  165.4 1.2 copy-start.5
  169.3 5.8 %copy-start.3 = (bf16[128,7168]{1,0:T(8,128)(2,1)S(1)}, bf16[128,7168]{1,0:T(8,128)(2,1)}, u32[]{:S(2)}) copy-start(bf16[128,7168]{1,0:T(8,128)(2,1)} %get-tuple-element.8) | copy-start | bytes 5505028
  181.7 20.7 %all-to-all-start.1 = ((bf16[32,8,512]{2,1,0:T(8,128)(2,1)}), bf16[32,8,512]{2,1,0:T(8,128)(2,1)S(1)}, u32[]{:S(2)}, u32[]{:S(2)}) async-start(bf16[32,8,512]{2,1,0:T(8,128)(2,1)} %pad_maximum_fusion.2), calls=%async_computation.2 | async-start | bytes 524288 | tf_op jit(solution)/shard_map/all_to_all | solution.py:62
  185.2 6.8 %copy-start.4 = (bf16[128,7168]{1,0:T(8,128)(2,1)S(1)}, bf16[128,7168]{1,0:T(8,128)(2,1)}, u32[]{:S(2)}) copy-start(bf16[128,7168]{1,0:T(8,128)(2,1)} %get-tuple-element.8) | copy-start | bytes 5505028
  192.0 12.2 %copy-start.1 = (bf16[8,4096]{1,0:T(8,128)(2,1)S(1)}, bf16[8,4096]{1,0:T(8,128)(2,1)}, u32[]{:S(2)}) copy-start(bf16[8,4096]{1,0:T(8,128)(2,1)} %param.8) | copy-start | bytes 196612
Sparse Core Ops, SparseCore 0:
  39.6 60.5 reduce-scatter.1
  101.8 56.6 all-gather.1
where the time goes:
time: 211 us
  waiting for transfers between devices  119 us (56%)
  matrix products  40.9 us (19%)
  blocking collectives  17.1 us (8%)
  between operations  14.3 us (7%)
  other arithmetic  12.2 us (6%)
  local copies, waits for them, and re-layouts  3.87 us (2%)
  starting transfers between devices  3.82 us (2%)
    reduce_scatter x1, waiting for transfers between devices, per_device(): summed = lax.psum_scatter(parts, 'shard', scatter_dimension=0, tiled=True)  60.5 us
    all_gather x1, waiting for transfers between devices, per_device(): lax.all_gather(summed, 'shard', axis=0, tiled=True).astype(jnp.float32)  58.3 us
    all_to_all x1, blocking collectives, per_device(): lax.all_to_all(jnp.concatenate([send(x_slots), send(d_slots)], axis=1), B...  17.1 us
    dot_general x3, matrix products, grad(): jnp.einsum('rd,rf->df', left, right, preferred_element_type=jnp.float32)  17.1 us
    dot_general x3, matrix products, back(): jnp.einsum('rf,df->rd', left, right, preferred_element_type=jnp.float32)  14 us
    dot_general x3, matrix products, partial(): jnp.dot(left, right, preferred_element_type=jnp.float32)  6.84 us
  transfers between devices with their start and end apart: 3, of which 2 were waited for; matrix products, arithmetic and copies ran while one was open for 8% of the time, Pallas kernels for 0%

commit v1 on v0

--- a/solution.py
+++ b/solution.py
@@ -1,10 +1,294 @@
+import functools
+
 import jax
 import jax.numpy as jnp
 from jax import lax
+from jax.experimental import pallas as pl
+from jax.experimental.pallas import tpu as pltpu
 from jax.sharding import PartitionSpec as P
 
 CAP = 4
 BOTH = ("expert", "shard")
+
+MESH = pl.DeviceIdType.MESH
+F32 = jnp.float32
+BF16 = jnp.bfloat16
+VMEM_BYTES = 60 * 2**20
+SKEW = 2
+
+
+def back(left, right):
+    return lax.dot_general(left, right, (((1,), (1,)), ((), ())), preferred_element_type=F32)
+
+
+def nonlinear(gate_value, up_value, d_hidden):
+    logistic = jax.nn.sigmoid(gate_value)
+    activation = gate_value * logistic
+    silu_slope = logistic * (1.0 + gate_value * (1.0 - logistic))
+    return (
+        (activation * up_value).astype(BF16),
+        (d_hidden * up_value * silu_slope).astype(BF16),
+        (d_hidden * activation).astype(BF16),
+    )
+
+
+def core_kernel(
+    chips, steps, width,
+    x_ref, d_ref, gate_hbm, up_hbm, down_hbm,
+    hidden_hbm, dgate_hbm, dup_hbm, out_ref, dexp_ref,
+    weights, pair_tx, pair_rx, local, p_tx, p_rx, s_tx, s_rx, act, out_acc, dexp_acc,
+    load_sem, pair_recv, p_recv, s_recv, act_recv, send_sem, store_sem,
+):
+    expert = lax.axis_index("expert")
+    shard = lax.axis_index("shard")
+    chip = shard // 2
+    core = shard % 2
+    mate = chip * 2 + 1 - core
+    last = chips - 1
+    right = lax.rem(shard + 2, 2 * chips)
+    left = lax.rem(shard + 2 * last, 2 * chips)
+    has_left = chip > 0
+    has_right = chip < last
+    lag_p = SKEW * chip
+    lag_s = SKEW * (last - chip)
+    lag = jnp.maximum(lag_p, lag_s)
+    sources = (gate_hbm, up_hbm, down_hbm)
+    targets = (hidden_hbm, dgate_hbm, dup_hbm)
+
+    def columns(q):
+        return pl.ds(pl.multiple_of(q * width, width), width)
+
+    def load(j, carry):
+        for side in (1 - core, core):
+            q = side * steps + j
+            for k in range(3):
+                pltpu.make_async_copy(
+                    sources[k].at[:, columns(q)], weights.at[q, k], load_sem.at[q]
+                ).start()
+        return carry
+
+    lax.fori_loop(0, steps, load, 0)
+
+    barrier = pltpu.get_barrier_semaphore()
+    pl.semaphore_signal(barrier, inc=1, device_id=(expert, mate), device_id_type=MESH)
+
+    @pl.when(has_left)
+    def _():
+        pl.semaphore_signal(barrier, inc=1, device_id=(expert, left), device_id_type=MESH)
+
+    @pl.when(has_right)
+    def _():
+        pl.semaphore_signal(barrier, inc=1, device_id=(expert, right), device_id_type=MESH)
+
+    @pl.when(jnp.logical_not(has_left))
+    def _():
+        p_rx[...] = jnp.zeros_like(p_rx)
+
+    @pl.when(jnp.logical_not(has_right))
+    def _():
+        s_rx[...] = jnp.zeros_like(s_rx)
+
+    out_acc[...] = jnp.zeros_like(out_acc)
+    dexp_acc[...] = jnp.zeros_like(dexp_acc)
+    pl.semaphore_wait(barrier, 1 + has_left.astype(jnp.int32) + has_right.astype(jnp.int32))
+
+    def remote(src, dst, send, recv, target):
+        return pltpu.make_async_remote_copy(
+            src_ref=src, dst_ref=dst, send_sem=send, recv_sem=recv,
+            device_id=(expert, target), device_id_type=MESH,
+        )
+
+    def pair_copy(j):
+        return remote(pair_tx.at[j], pair_rx.at[j], send_sem.at[0], pair_recv.at[j], mate)
+
+    def p_copy(j, k):
+        return remote(p_tx.at[j, k], p_rx.at[j, k], send_sem.at[1], p_recv.at[j * 3 + k], right)
+
+    def s_copy(j, k):
+        return remote(s_tx.at[j, k], s_rx.at[j, k], send_sem.at[2], s_recv.at[j * 3 + k], left)
+
+    def act_copy(j, side):
+        q = side * steps + j
+        return remote(act.at[q], act.at[q], send_sem.at[3], act_recv.at[j], mate)
+
+    def partial(q, k):
+        rows = d_ref if k == 2 else x_ref
+        return jnp.dot(rows[...], weights[q, k], preferred_element_type=F32)
+
+    def store(q):
+        for k in range(3):
+            pltpu.make_async_copy(act.at[q, k], targets[k].at[:, columns(q)], store_sem).start()
+
+    def backward(q):
+        out_acc[...] += back(act[q, 0], weights[q, 2])
+        dexp_acc[...] += back(act[q, 1], weights[q, 0]) + back(act[q, 2], weights[q, 1])
+
+    def within(j):
+        return jnp.logical_and(j >= 0, j < steps)
+
+    def tick(t, carry):
+        @pl.when(t < steps)
+        def _():
+            for side in (1 - core, core):
+                q = side * steps + t
+                pltpu.make_async_copy(weights.at[q], weights.at[q], load_sem.at[q]).wait()
+            q = (1 - core) * steps + t
+            for k in range(3):
+                pair_tx[t, k] = partial(q, k).astype(BF16)
+            pair_copy(t).start()
+            q = core * steps + t
+            for k in range(3):
+                local[t, k] = partial(q, k)
+
+        j = t - 1
+
+        @pl.when(within(j))
+        def _():
+            pair_copy(j).wait_recv()
+            for k in range(3):
+                local[j, k] += pair_rx[j, k].astype(F32)
+
+        jp = t - 1 - lag_p
+
+        @pl.when(within(jp))
+        def _():
+            for k in range(3):
+                @pl.when(has_left)
+                def _():
+                    p_copy(jp, k).wait_recv()
+
+                @pl.when(has_right)
+                def _():
+                    p_tx[jp, k] = (local[jp, k] + p_rx[jp, k].astype(F32)).astype(BF16)
+                    p_copy(jp, k).start()
+
+        js = t - 1 - lag_s
+
+        @pl.when(within(js))
+        def _():
+            for k in range(3):
+                @pl.when(has_right)
+                def _():
+                    s_copy(js, k).wait_recv()
+
+                @pl.when(has_left)
+                def _():
+                    s_tx[js, k] = (local[js, k] + s_rx[js, k].astype(F32)).astype(BF16)
+                    s_copy(js, k).start()
+
+        jf = t - 1 - lag
+
+        @pl.when(within(jf))
+        def _():
+            q = core * steps + jf
+            total = [
+                local[jf, k] + p_rx[jf, k].astype(F32) + s_rx[jf, k].astype(F32) for k in range(3)
+            ]
+            for k, value in enumerate(nonlinear(*total)):
+                act[q, k] = value
+            act_copy(jf, core).start()
+            store(q)
+            backward(q)
+
+        jb = jf - 1
+
+        @pl.when(within(jb))
+        def _():
+            q = (1 - core) * steps + jb
+            act_copy(jb, 1 - core).wait_recv()
+            store(q)
+            backward(q)
+
+        return carry
+
+    lax.fori_loop(0, steps + SKEW * last + 2, tick, 0)
+    out_ref[...] = out_acc[...].astype(BF16)
+    dexp_ref[...] = dexp_acc[...].astype(BF16)
+    remote(pair_tx, pair_rx, send_sem.at[0], pair_recv.at[0], mate).wait_send()
+
+    @pl.when(has_right)
+    def _():
+        remote(p_tx, p_rx, send_sem.at[1], p_recv.at[0], right).wait_send()
+
+    @pl.when(has_left)
+    def _():
+        remote(s_tx, s_rx, send_sem.at[2], s_recv.at[0], left).wait_send()
+
+    half = act.at[pl.ds(0, steps)]
+    remote(half, half, send_sem.at[3], act_recv.at[0], mate).wait_send()
+    pltpu.make_async_copy(act, act, store_sem).wait()
+
+
+def plan(shards, rows, part, units):
+    if shards % 2 or units % 256:
+        return None
+    for width in (256, 128):
+        if (units // 2) % width:
+            continue
+        held = 3 * part * units * 2 + 3 * rows * units * (2 + 2 + 6 * 1) + 2 * rows * part * (4 + 8)
+        if held <= 55 * 2**20:
+            return width
+    return None
+
+
+def expert_core(x_rows, d_rows, w_gate, w_up, w_down, width):
+    shards = lax.axis_size("shard")
+    rows, part = x_rows.shape
+    units = w_gate.shape[1]
+    steps = units // 2 // width
+    chips = shards // 2
+    anywhere = pl.BlockSpec(memory_space=pl.ANY)
+    vmem = pl.BlockSpec(memory_space=pltpu.VMEM)
+    block = (steps, 3, rows, width)
+    dma = pltpu.SemaphoreType.DMA
+    return pl.pallas_call(
+        functools.partial(core_kernel, chips, steps, width),
+        out_shape=[jax.ShapeDtypeStruct((rows, units), BF16)] * 3
+        + [jax.ShapeDtypeStruct((rows, part), BF16)] * 2,
+        in_specs=[vmem] * 2 + [anywhere] * 3,
+        out_specs=[anywhere] * 3 + [vmem] * 2,
+        scratch_shapes=[
+            pltpu.VMEM((2 * steps, 3, part, width), BF16),
+            pltpu.VMEM(block, BF16),
+            pltpu.VMEM(block, BF16),
+            pltpu.VMEM(block, F32),
+            pltpu.VMEM(block, BF16),
+            pltpu.VMEM(block, BF16),
+            pltpu.VMEM(block, BF16),
+            pltpu.VMEM(block, BF16),
+            pltpu.VMEM((2 * steps, 3, rows, width), BF16),
+            pltpu.VMEM((rows, part), F32),
+            pltpu.VMEM((rows, part), F32),
+            dma((2 * steps,)),
+            dma((steps,)),
+            dma((3 * steps,)),
+            dma((3 * steps,)),
+            dma((steps,)),
+            dma((4,)),
+            dma,
+        ],
+        compiler_params=pltpu.CompilerParams(
+            collective_id=0, has_side_effects=True, vmem_limit_bytes=VMEM_BYTES
+        ),
+        name="expert_core",
+    )(x_rows, d_rows, w_gate, w_up, w_down)
+
+
+def expert_plain(x_rows, d_rows, w_gate, w_up, w_down):
+    rows = x_rows.shape[0]
+
+    def partial(left, right):
+        return jnp.dot(left, right, preferred_element_type=F32).astype(BF16)
+
+    parts = jnp.concatenate(
+        [partial(x_rows, w_gate), partial(x_rows, w_up), partial(d_rows, w_down)], axis=0
+    )
+    summed = lax.psum_scatter(parts, "shard", scatter_dimension=0, tiled=True)
+    full = lax.all_gather(summed, "shard", axis=0, tiled=True).astype(F32)
+    hidden, d_gate, d_up = nonlinear(full[:rows], full[rows : 2 * rows], full[2 * rows :])
+    expert_out = back(hidden, w_down).astype(BF16)
+    d_expert = (back(d_gate, w_gate) + back(d_up, w_up)).astype(BF16)
+    return hidden, d_gate, d_up, expert_out, d_expert
 
 
 def per_device(tokens, cotangent, expert_ids, slot_ids, route_weight, w_gate, w_up, w_down):
@@ -38,27 +322,15 @@
     d_rows = arrived[:, CAP:].reshape(rows, part)
     hidden_units = w_gate.shape[2]
 
-    def partial(left, right):
-        return jnp.dot(left, right, preferred_element_type=jnp.float32).astype(jnp.bfloat16)
-
-    parts = jnp.concatenate(
-        [partial(x_rows, w_gate[0]), partial(x_rows, w_up[0]), partial(d_rows, w_down[0])], axis=0
-    )
-    summed = lax.psum_scatter(parts, "shard", scatter_dimension=0, tiled=True)
-    full = lax.all_gather(summed, "shard", axis=0, tiled=True).astype(jnp.float32)
-    gate_value, up_value, d_hidden = full[:rows], full[rows : 2 * rows], full[2 * rows :]
-    logistic = jax.nn.sigmoid(gate_value)
-    activation = gate_value * logistic
-    silu_slope = logistic * (1.0 + gate_value * (1.0 - logistic))
-    hidden = (activation * up_value).astype(jnp.bfloat16)
-    d_gate = (d_hidden * up_value * silu_slope).astype(jnp.bfloat16)
-    d_up = (d_hidden * activation).astype(jnp.bfloat16)
-
-    def back(left, right):
-        return jnp.einsum("rf,df->rd", left, right, preferred_element_type=jnp.float32)
-
-    expert_out = back(hidden, w_down[0]).astype(jnp.bfloat16)
-    d_expert = (back(d_gate, w_gate[0]) + back(d_up, w_up[0])).astype(jnp.bfloat16)
+    width_step = plan(shards, rows, part, hidden_units)
+    if width_step:
+        hidden, d_gate, d_up, expert_out, d_expert = expert_core(
+            x_rows, d_rows, w_gate[0], w_up[0], w_down[0], width_step
+        )
+    else:
+        hidden, d_gate, d_up, expert_out, d_expert = expert_plain(
+            x_rows, d_rows, w_gate[0], w_up[0], w_down[0]
+        )
     returned = lax.all_to_all(
         jnp.concatenate(
             [expert_out.reshape(-1, CAP, part), d_expert.reshape(-1, CAP, part)], axis=1

time: 211 us -> 131 us (0.62)
  waiting for transfers between devices: 119 us -> 0.01 us
  Pallas kernels: 0 us -> 83.2 us
  matrix products: 40.9 us -> 20 us
  between operations: 14.3 us -> 0.79 us
  other arithmetic: 12.2 us -> 2.46 us
    pallas_call x0 -> x1, Pallas kernels: none -> 83.2 us  [expert_core(): pl.pallas_call(functools.partial(core_kernel, chips, steps, width), out_s...]
    reduce_scatter x1 -> x0, waiting for transfers between devices: 60.5 us -> none  [per_device(): summed = lax.psum_scatter(parts, 'shard', scatter_dimension=0, tiled=True)]
    all_gather x1 -> x0, waiting for transfers between devices: 58.3 us -> none  [per_device(): lax.all_gather(summed, 'shard', axis=0, tiled=True).astype(jnp.float32)]
    dot_general x6 -> x0, matrix products: 20.9 us -> none  [the longest x3 14 us: back(): jnp.einsum('rf,df->rd', left, right, preferred_element_type=jnp.float32)]
    convert_element_type x2 -> x0, other arithmetic: 6.94 us -> none  [the longest x1 4.06 us: per_device(): lax.all_gather(summed, 'shard', axis=0, tiled=True).astype(jnp.float32)]
    unnamed x26 -> x14, local copies, waits for them, and re-layouts: 3.36 us -> 0.2 us
    concatenate x1 -> x0, other arithmetic: 2.97 us -> none  [per_device(): jnp.concatenate([partial(x_rows, w_gate[0]), partial(x_rows, w_up[0]), pa...]
  transfers between devices with their start and end apart: 3 -> 1, of which waited for: 2 -> 0; matrix products, arithmetic and copies ran while one was open for 8% -> 13% of each run, Pallas kernels for 0% -> 0%
where the time goes in v1:
time: 131 us; the launch traced here: 130 us
  Pallas kernels  83.2 us (64%)
  matrix products  20 us (15%)
  blocking collectives  17.1 us (13%)
  local copies, waits for them, and re-layouts  3.99 us (3%)
  starting transfers between devices  2.58 us (2%)
  other arithmetic  2.46 us (2%)
    pallas_call x1, Pallas kernels, expert_core(): pl.pallas_call(functools.partial(core_kernel, chips, steps, width), out_s...  83.2 us
    all_to_all x1, blocking collectives, per_device(): lax.all_to_all(jnp.concatenate([send(x_slots), send(d_slots)], axis=1), B...  17.1 us
    dot_general x3, matrix products, grad(): jnp.einsum('rd,rf->df', left, right, preferred_element_type=jnp.float32)  17.1 us
  transfers between devices with their start and end apart: 1, of which 0 were waited for; matrix products, arithmetic and copies ran while one was open for 13% of the time, Pallas kernels for 0%

profile of v1, /device:TPU:0, one launch (start us, length us, event | category | flops | bytes accessed | tf_op | source)
XLA Modules:
  0.0 130.2 jit_solution(12628324242488681368)
XLA Ops:
  0.6 0.0 copy-start
  0.6 0.7 multiply_add_fusion
  1.4 0.8 convert_reduce_fusion
  2.1 0.0 copy-done
  2.1 0.2 convolution_convert_fusion.4
  2.4 0.1 copy.37
  2.5 1.2 convolution_convert_fusion.3
  3.7 0.1 copy.38
  3.8 0.1 pad_maximum_fusion
  3.9 17.1 %all_to_all.10 = bf16[32,8,512]{2,1,0:T(8,128)(2,1)S(1)} all-to-all(bf16[32,8,512]{2,1,0:T(8,128)(2,1)S(1)} %pad_maximum_fusion), channel_id=1, replica_groups=mesh['expert'=4,'shard'=8] {'expert','shard'}, dimensions={0} | all-to-all | bytes 524288 | tf_op jit(solution)/shard_map/all_to_all | solution.py:317
  21.1 0.1 fusion.6
  21.1 0.7 reshape.53.d_ref
  21.8 0.7 reshape.52.x_ref
  22.5 83.2 %expert_core.1 = (bf16[128,7168]{1,0:T(8,128)(2,1)}, bf16[128,7168]{1,0:T(8,128)(2,1)}, bf16[128,7168]{1,0:T(8,128)(2,1)}, bf16[128,512]{1,0:T(8,128)(2,1)}, bf16[128,512]{1,0:T(8,128)(2,1)}) custom-call(bf16[128,512]{1,0:T(8,128)(2,1)} %reshape.52.x_ref, bf16[128,512]{1,0:T(8,128)(2,1)} %reshape.53.d_ref, bf16[512,7168]{1,0:T(8,128)(2,1)} %bitcast.49, ...), custom_call_target="tpu_custom_call" | custom-call | tf_op jit(solution)/shard_map/expert_core/pallas_call | solution.py:244
  105.7 0.0 copy-start.1
  105.7 0.0 copy-start.3
  105.7 1.1 reshape.54
  106.8 0.9 reshape.55
  107.8 0.8 pad_maximum_fusion.1
  108.6 2.6 %all-to-all-start.1 = ((bf16[32,8,512]{2,1,0:T(8,128)(2,1)}), bf16[32,8,512]{2,1,0:T(8,128)(2,1)S(1)}, u32[]{:S(2)}, u32[]{:S(2)}) async-start(bf16[32,8,512]{2,1,0:T(8,128)(2,1)} %pad_maximum_fusion.1), calls=%async_computation.1 | async-start | bytes 524288 | tf_op jit(solution)/shard_map/all_to_all | solution.py:334
  111.2 0.0 copy-done.4
  111.2 0.0 copy-start.2
  111.2 6.8 %fusion.2 = bf16[1,512,7168]{2,1,0:T(8,128)(2,1)} fusion(bf16[128,512]{1,0:T(8,128)(2,1)S(1)} %copy-done.4, bf16[128,7168]{1,0:T(8,128)(2,1)} %get-tuple-element.14), kind=kOutput, calls=%fused_computation.5 | convolution fusion | flops 943194112 | bytes 9306112 | tf_op jit(solution)/shard_map/rd,rf->df/dot_general | solution.py:352
  118.0 0.0 copy-done.1
  118.0 0.0 copy-done.3
  118.0 5.1 %fusion = bf16[1,512,7168]{2,1,0:T(8,128)(2,1)} fusion(bf16[128,512]{1,0:T(8,128)(2,1)S(1)} %copy-done.1, bf16[128,7168]{1,0:T(8,128)(2,1)S(1)} %copy-done.3), kind=kOutput, calls=%fused_computation.3 | convolution fusion | flops 943194112 | bytes 9306112 | tf_op jit(solution)/shard_map/rd,rf->df/dot_general | solution.py:352
  123.1 0.0 copy-done.2
  123.1 5.1 %fusion.1 = bf16[1,512,7168]{2,1,0:T(8,128)(2,1)} fusion(bf16[128,512]{1,0:T(8,128)(2,1)S(1)} %copy-done.1, bf16[128,7168]{1,0:T(8,128)(2,1)S(1)} %copy-done.2), kind=kOutput, calls=%fused_computation.4 | convolution fusion | flops 943194112 | bytes 9306112 | tf_op jit(solution)/shard_map/rd,rf->df/dot_general | solution.py:352
  128.3 0.0 all-to-all-done.1
  128.3 0.1 fusion.5
  128.5 0.8 convolution_convert_fusion.5
  129.4 0.8 convolution_convert_fusion.6
  (8 shorter events, 0.2 us)
Async XLA Ops:
  0.6 1.5 %copy-start = (bf16[8,4096]{1,0:T(8,128)(2,1)S(1)}, bf16[8,4096]{1,0:T(8,128)(2,1)}, u32[]{:S(2)}) copy-start(bf16[8,4096]{1,0:T(8,128)(2,1)} %param.8) | copy-start | bytes 196612
  22.5 88.7 %copy-start.4 = (bf16[128,512]{1,0:T(8,128)(2,1)S(1)}, bf16[128,512]{1,0:T(8,128)(2,1)}, u32[]{:S(2)}) copy-start(bf16[128,512]{1,0:T(8,128)(2,1)} %reshape.53.d_ref) | copy-start | bytes 393220
  105.7 12.3 %copy-start.1 = (bf16[128,512]{1,0:T(8,128)(2,1)S(1)}, bf16[128,512]{1,0:T(8,128)(2,1)}, u32[]{:S(2)}) copy-start(bf16[128,512]{1,0:T(8,128)(2,1)} %reshape.52.x_ref) | copy-start | bytes 393220
  105.7 12.3 %copy-start.3 = (bf16[128,7168]{1,0:T(8,128)(2,1)S(1)}, bf16[128,7168]{1,0:T(8,128)(2,1)}, u32[]{:S(2)}) copy-start(bf16[128,7168]{1,0:T(8,128)(2,1)} %get-tuple-element.12) | copy-start | bytes 5505028
  108.6 19.7 %all-to-all-start.1 = ((bf16[32,8,512]{2,1,0:T(8,128)(2,1)}), bf16[32,8,512]{2,1,0:T(8,128)(2,1)S(1)}, u32[]{:S(2)}, u32[]{:S(2)}) async-start(bf16[32,8,512]{2,1,0:T(8,128)(2,1)} %pad_maximum_fusion.1), calls=%async_computation.1 | async-start | bytes 524288 | tf_op jit(solution)/shard_map/all_to_all | solution.py:334
  111.2 11.9 %copy-start.2 = (bf16[128,7168]{1,0:T(8,128)(2,1)S(1)}, bf16[128,7168]{1,0:T(8,128)(2,1)}, u32[]{:S(2)}) copy-start(bf16[128,7168]{1,0:T(8,128)(2,1)} %get-tuple-element.13) | copy-start | bytes 5505028

commit v2 on v1

--- a/solution.py
+++ b/solution.py
@@ -34,16 +34,19 @@
 
 def core_kernel(
     chips, steps, width,
-    x_ref, d_ref, gate_hbm, up_hbm, down_hbm,
-    hidden_hbm, dgate_hbm, dup_hbm, out_ref, dexp_ref,
-    weights, pair_tx, pair_rx, local, p_tx, p_rx, s_tx, s_rx, act, out_acc, dexp_acc,
-    load_sem, pair_recv, p_recv, s_recv, act_recv, send_sem, store_sem,
+    pieces_ref, gate_hbm, up_hbm, down_hbm,
+    hidden_hbm, dgate_hbm, dup_hbm, x_ref, d_ref, results_ref,
+    pieces_rx, weights, pair_tx, pair_rx, local, p_tx, p_rx, s_tx, s_rx, act, out_acc, dexp_acc,
+    load_sem, piece_recv, pair_recv, p_recv, s_recv, act_recv, send_sem, store_sem,
 ):
     expert = lax.axis_index("expert")
     shard = lax.axis_index("shard")
     chip = shard // 2
     core = shard % 2
     mate = chip * 2 + 1 - core
+    shards = 2 * chips
+    me = expert * shards + shard
+    devices = pieces_ref.shape[0]
     last = chips - 1
     right = lax.rem(shard + 2, 2 * chips)
     left = lax.rem(shard + 2 * last, 2 * chips)
@@ -70,15 +73,15 @@
     lax.fori_loop(0, steps, load, 0)
 
     barrier = pltpu.get_barrier_semaphore()
-    pl.semaphore_signal(barrier, inc=1, device_id=(expert, mate), device_id_type=MESH)
-
-    @pl.when(has_left)
-    def _():
-        pl.semaphore_signal(barrier, inc=1, device_id=(expert, left), device_id_type=MESH)
-
-    @pl.when(has_right)
-    def _():
-        pl.semaphore_signal(barrier, inc=1, device_id=(expert, right), device_id_type=MESH)
+
+    def greet(o, carry):
+        other = lax.rem(me + o, devices)
+        pl.semaphore_signal(
+            barrier, inc=1, device_id=(other // shards, other % shards), device_id_type=MESH
+        )
+        return carry
+
+    lax.fori_loop(1, devices, greet, 0)
 
     @pl.when(jnp.logical_not(has_left))
     def _():
@@ -90,13 +93,50 @@
 
     out_acc[...] = jnp.zeros_like(out_acc)
     dexp_acc[...] = jnp.zeros_like(dexp_acc)
-    pl.semaphore_wait(barrier, 1 + has_left.astype(jnp.int32) + has_right.astype(jnp.int32))
+    pieces_rx[me] = pieces_ref[me]
+    pl.semaphore_wait(barrier, devices - 1)
 
     def remote(src, dst, send, recv, target):
         return pltpu.make_async_remote_copy(
             src_ref=src, dst_ref=dst, send_sem=send, recv_sem=recv,
             device_id=(expert, target), device_id_type=MESH,
         )
+
+    def piece_copy(target, source):
+        return pltpu.make_async_remote_copy(
+            src_ref=pieces_ref.at[target], dst_ref=pieces_rx.at[source],
+            send_sem=send_sem.at[4], recv_sem=piece_recv.at[source],
+            device_id=(target // shards, target % shards), device_id_type=MESH,
+        )
+
+    def send_piece(o, carry):
+        piece_copy(lax.rem(me + o, devices), me).start()
+        return carry
+
+    def await_piece(o, carry):
+        other = lax.rem(me + o, devices)
+        piece_copy(other, other).wait_recv()
+        return carry
+
+    lax.fori_loop(1, devices, send_piece, 0)
+    lax.fori_loop(1, devices, await_piece, 0)
+    tile_rows, half = pieces_ref.shape[1:]
+    rows = devices * CAP
+    mixed = pieces_rx[...].reshape(devices * tile_rows, half)
+    halves = tile_rows // (2 * CAP)
+
+    def picks(kind, h, transposed):
+        shape = (devices * tile_rows, rows) if transposed else (rows, devices * tile_rows)
+        slot = lax.broadcasted_iota(jnp.int32, shape, int(transposed))
+        piece = lax.broadcasted_iota(jnp.int32, shape, 1 - int(transposed))
+        wanted = slot // CAP * tile_rows + h * 2 * CAP + kind * CAP + slot % CAP
+        return (piece == wanted).astype(F32).astype(BF16)
+
+    for kind, ref in enumerate((x_ref, d_ref)):
+        for h in range(halves):
+            ref[:, h * half : (h + 1) * half] = jnp.dot(
+                picks(kind, h, False), mixed, preferred_element_type=F32
+            ).astype(BF16)
 
     def pair_copy(j):
         return remote(pair_tx.at[j], pair_rx.at[j], send_sem.at[0], pair_recv.at[j], mate)
@@ -202,8 +242,21 @@
         return carry
 
     lax.fori_loop(0, steps + SKEW * last + 2, tick, 0)
-    out_ref[...] = out_acc[...].astype(BF16)
-    dexp_ref[...] = dexp_acc[...].astype(BF16)
+    total = jnp.zeros((devices * tile_rows, half), F32)
+    for kind, acc in enumerate((out_acc, dexp_acc)):
+        for h in range(halves):
+            total += jnp.dot(
+                picks(kind, h, True),
+                acc[:, h * half : (h + 1) * half].astype(BF16),
+                preferred_element_type=F32,
+            )
+    results_ref[...] = total.astype(BF16).reshape(results_ref.shape)
+    sent = pl.ds(0, devices - 1)
+    pltpu.make_async_remote_copy(
+        src_ref=pieces_ref.at[sent], dst_ref=pieces_rx.at[sent],
+        send_sem=send_sem.at[4], recv_sem=piece_recv.at[0],
+        device_id=(expert, mate), device_id_type=MESH,
+    ).wait_send()
     remote(pair_tx, pair_rx, send_sem.at[0], pair_recv.at[0], mate).wait_send()
 
     @pl.when(has_right)
@@ -214,13 +267,13 @@
     def _():
         remote(s_tx, s_rx, send_sem.at[2], s_recv.at[0], left).wait_send()
 
-    half = act.at[pl.ds(0, steps)]
-    remote(half, half, send_sem.at[3], act_recv.at[0], mate).wait_send()
+    mine = act.at[pl.ds(0, steps)]
+    remote(mine, mine, send_sem.at[3], act_recv.at[0], mate).wait_send()
     pltpu.make_async_copy(act, act, store_sem).wait()
 
 
 def plan(shards, rows, part, units):
-    if shards % 2 or units % 256:
+    if shards % 2 or units % 256 or part % (16 // (2 * CAP) * 128):
         return None
     for width in (256, 128):
         if (units // 2) % width:
@@ -231,10 +284,11 @@
     return None
 
 
-def expert_core(x_rows, d_rows, w_gate, w_up, w_down, width):
+def expert_core(pieces, w_gate, w_up, w_down, width):
     shards = lax.axis_size("shard")
-    rows, part = x_rows.shape
-    units = w_gate.shape[1]
+    devices = pieces.shape[0]
+    rows = devices * CAP
+    part, units = w_gate.shape
     steps = units // 2 // width
     chips = shards // 2
     anywhere = pl.BlockSpec(memory_space=pl.ANY)
@@ -244,10 +298,12 @@
     return pl.pallas_call(
         functools.partial(core_kernel, chips, steps, width),
         out_shape=[jax.ShapeDtypeStruct((rows, units), BF16)] * 3
-        + [jax.ShapeDtypeStruct((rows, part), BF16)] * 2,
-        in_specs=[vmem] * 2 + [anywhere] * 3,
-        out_specs=[anywhere] * 3 + [vmem] * 2,
+        + [jax.ShapeDtypeStruct((rows, part), BF16)] * 2
+        + [jax.ShapeDtypeStruct(pieces.shape, BF16)],
+        in_specs=[vmem] + [anywhere] * 3,
+        out_specs=[anywhere] * 3 + [vmem] * 3,
         scratch_shapes=[
+            pltpu.VMEM(pieces.shape, BF16),
             pltpu.VMEM((2 * steps, 3, part, width), BF16),
             pltpu.VMEM(block, BF16),
             pltpu.VMEM(block, BF16),
@@ -260,18 +316,19 @@
             pltpu.VMEM((rows, part), F32),
             pltpu.VMEM((rows, part), F32),
             dma((2 * steps,)),
+            dma((devices,)),
             dma((steps,)),
             dma((3 * steps,)),
             dma((3 * steps,)),
             dma((steps,)),
-            dma((4,)),
+            dma((5,)),
             dma,
         ],
         compiler_params=pltpu.CompilerParams(
             collective_id=0, has_side_effects=True, vmem_limit_bytes=VMEM_BYTES
         ),
         name="expert_core",
-    )(x_rows, d_rows, w_gate, w_up, w_down)
+    )(pieces, w_gate, w_up, w_down)
 
 
 def expert_plain(x_rows, d_rows, w_gate, w_up, w_down):
@@ -310,42 +367,39 @@
         combine.T, cotangent.astype(jnp.float32), precision=lax.Precision.HIGHEST
     ).astype(jnp.bfloat16)
 
-    def send(slots):
-        pieces = slots.reshape(experts, CAP, shards, part).transpose(0, 2, 1, 3)
-        return pieces.reshape(experts * shards, CAP, part)
-
-    arrived = lax.all_to_all(
-        jnp.concatenate([send(x_slots), send(d_slots)], axis=1),
-        BOTH, split_axis=0, concat_axis=0, tiled=True,
-    )
-    x_rows = arrived[:, :CAP].reshape(rows, part)
-    d_rows = arrived[:, CAP:].reshape(rows, part)
     hidden_units = w_gate.shape[2]
-
+    devices = experts * shards
     width_step = plan(shards, rows, part, hidden_units)
+    halves = 16 // (2 * CAP) if width_step else 1
+
+    both = jnp.stack([x_slots, d_slots]).reshape(
+        2, experts, CAP, shards, halves, part // halves
+    )
+    pieces = both.transpose(1, 3, 4, 0, 2, 5).reshape(
+        devices, halves * 2 * CAP, part // halves
+    )
     if width_step:
-        hidden, d_gate, d_up, expert_out, d_expert = expert_core(
-            x_rows, d_rows, w_gate[0], w_up[0], w_down[0], width_step
+        hidden, d_gate, d_up, x_rows, d_rows, results = expert_core(
+            pieces, w_gate[0], w_up[0], w_down[0], width_step
         )
     else:
+        arrived = lax.all_to_all(pieces, BOTH, split_axis=0, concat_axis=0, tiled=True)
+        x_rows = arrived[:, :CAP].reshape(rows, part)
+        d_rows = arrived[:, CAP:].reshape(rows, part)
         hidden, d_gate, d_up, expert_out, d_expert = expert_plain(
             x_rows, d_rows, w_gate[0], w_up[0], w_down[0]
         )
-    returned = lax.all_to_all(
-        jnp.concatenate(
+        results = jnp.concatenate(
             [expert_out.reshape(-1, CAP, part), d_expert.reshape(-1, CAP, part)], axis=1
-        ),
-        BOTH, split_axis=0, concat_axis=0, tiled=True,
-    )
-
-    def take(pieces):
-        return pieces.reshape(experts, shards, CAP, part).transpose(0, 2, 1, 3).reshape(slots_all, width)
-
+        )
+    returned = lax.all_to_all(results, BOTH, split_axis=0, concat_axis=0, tiled=True)
+    returned = returned.reshape(experts, shards, halves, 2, CAP, part // halves)
+    returned = returned.transpose(3, 0, 4, 1, 2, 5).reshape(2, slots_all, width)
     layer_out = jnp.dot(
-        combine, take(returned[:, :CAP]).astype(jnp.float32), precision=lax.Precision.HIGHEST
+        combine, returned[0].astype(jnp.float32), precision=lax.Precision.HIGHEST
     ).astype(jnp.bfloat16)
     d_tokens = jnp.dot(
-        dispatch, take(returned[:, CAP:]), preferred_element_type=jnp.float32
+        dispatch, returned[1], preferred_element_type=jnp.float32
     ).astype(jnp.bfloat16)
 
     def grad(left, right):

time: 131 us -> 124 us (0.947)
  blocking collectives: 17.1 us -> 0 us
  Pallas kernels: 83.2 us -> 96.9 us
  local copies, waits for them, and re-layouts: 3.99 us -> 1.72 us
    all_to_all x1 -> x0, blocking collectives: 17.1 us -> none  [per_device(): lax.all_to_all(jnp.concatenate([send(x_slots), send(d_slots)], axis=1), B...]
    pallas_call x1, Pallas kernels: 83.2 us -> 96.9 us  [expert_core(): pl.pallas_call(functools.partial(core_kernel, chips, steps, width), out_s...]
    reshape x4 -> x3, local copies, waits for them, and re-layouts: 3.4 us -> 1.06 us  [the longest x1 0.77 us: per_device(): both.transpose(1, 3, 4, 0, 2, 5)]
  transfers between devices with their start and end apart: 1 -> 1, of which waited for: 0 -> 0; matrix products, arithmetic and copies ran while one was open for 13% -> 14% of each run, Pallas kernels for 0% -> 0%
where the time goes in v2:
time: 124 us
  Pallas kernels  96.9 us (78%)
  matrix products  20.1 us (16%)
  starting transfers between devices  2.73 us (2%)
  local copies, waits for them, and re-layouts  1.72 us (1%)
  other arithmetic  1.66 us (1%)
    pallas_call x1, Pallas kernels, expert_core(): pl.pallas_call(functools.partial(core_kernel, chips, steps, width), out_s...  96.9 us
    dot_general x3, matrix products, grad(): jnp.einsum('rd,rf->df', left, right, preferred_element_type=jnp.float32)  17.1 us
    all_to_all x1, starting transfers between devices, per_device(): lax.all_to_all(results, BOTH, split_axis=0, concat_axis=0, tiled=True)  2.73 us
  transfers between devices with their start and end apart: 1, of which 0 were waited for; matrix products, arithmetic and copies ran while one was open for 14% of the time, Pallas kernels for 0%

profile of v2, /device:TPU:0, one launch (start us, length us, event | category | flops | bytes accessed | tf_op | source)
XLA Modules:
  0.0 123.9 jit_solution(6041334050559346773)
XLA Ops:
  0.6 0.0 copy-start
  0.6 0.7 multiply_add_fusion
  1.4 0.8 convert_reduce_fusion
  2.1 0.0 copy-done
  2.1 0.2 convolution_convert_fusion.4
  2.4 0.1 stack.9
  2.4 0.1 copy.22
  2.5 1.2 convolution_convert_fusion.3
  3.7 0.1 stack.10
  3.8 0.1 copy.23
  3.8 0.2 maximum_bitcast_fusion
  4.0 0.8 reshape.28.pieces_ref
  4.8 96.9 %expert_core.1 = (bf16[128,7168]{1,0:T(8,128)(2,1)}, bf16[128,7168]{1,0:T(8,128)(2,1)}, bf16[128,7168]{1,0:T(8,128)(2,1)}, bf16[128,512]{1,0:T(8,128)(2,1)}, bf1...) custom-call(bf16[32,16,256]{2,1,0:T(8,128)(2,1)} %reshape.28.pieces_ref, bf16[512,7168]{1,0:T(8,128)(2,1)} %bitcast.28, ...), custom_call_target="tpu_custom_call" | custom-call | tf_op jit(solution)/shard_map/expert_core/pallas_call | solution.py:298
  101.7 0.0 copy-start.2
  101.7 0.0 copy-start.3
  101.7 2.7 %all-to-all-start = ((bf16[32,16,256]{2,1,0:T(8,128)(2,1)}), bf16[32,16,256]{2,1,0:T(8,128)(2,1)S(1)}, u32[]{:S(2)}, u32[]{:S(2)}) async-start(bf16[32,16,256]{2,1,0:T(8,128)(2,1)} %get-tuple-element.11), calls=%async_computation | async-start | bytes 524288 | tf_op jit(solution)/shard_map/all_to_all | solution.py:395
  104.5 0.0 copy-start.1
  104.5 0.0 copy-start.4
  104.5 6.8 %fusion = bf16[1,512,7168]{2,1,0:T(8,128)(2,1)} fusion(bf16[128,512]{1,0:T(8,128)(2,1)} %get-tuple-element.12, bf16[128,7168]{1,0:T(8,128)(2,1)} %get-tuple-element.13), kind=kOutput, calls=%fused_computation.3 | convolution fusion | flops 943194112 | bytes 9306112 | tf_op jit(solution)/shard_map/rd,rf->df/dot_general | solution.py:406
  111.4 0.0 copy-done.2
  111.4 0.0 copy-done.3
  111.4 5.1 %fusion.1 = bf16[1,512,7168]{2,1,0:T(8,128)(2,1)} fusion(bf16[128,512]{1,0:T(8,128)(2,1)S(1)} %copy-done.3, bf16[128,7168]{1,0:T(8,128)(2,1)S(1)} %copy-done.2), kind=kOutput, calls=%fused_computation.4 | convolution fusion | flops 943194112 | bytes 9306112 | tf_op jit(solution)/shard_map/rd,rf->df/dot_general | solution.py:406
  116.5 0.0 copy-done.1
  116.5 5.1 %fusion.2 = bf16[1,512,7168]{2,1,0:T(8,128)(2,1)} fusion(bf16[128,512]{1,0:T(8,128)(2,1)S(1)} %copy-done.4, bf16[128,7168]{1,0:T(8,128)(2,1)S(1)} %copy-done.1), kind=kOutput, calls=%fused_computation.5 | convolution fusion | flops 943194112 | bytes 9306112 | tf_op jit(solution)/shard_map/rd,rf->df/dot_general | solution.py:406
  121.7 0.0 all-to-all-done
  121.7 0.1 reshape.29
  121.7 0.2 copy.26
  122.0 0.2 fusion.5
  122.2 0.1 squeeze.19
  122.2 0.8 convolution_convert_fusion.5
  123.0 0.1 squeeze.18
  123.1 0.8 convolution_convert_fusion.6
  (1 shorter events, 0.0 us)
Async XLA Ops:
  0.6 1.5 %copy-start = (bf16[8,4096]{1,0:T(8,128)(2,1)S(1)}, bf16[8,4096]{1,0:T(8,128)(2,1)}, u32[]{:S(2)}) copy-start(bf16[8,4096]{1,0:T(8,128)(2,1)} %param.8) | copy-start | bytes 196612
  101.7 9.6 %copy-start.2 = (bf16[128,7168]{1,0:T(8,128)(2,1)S(1)}, bf16[128,7168]{1,0:T(8,128)(2,1)}, u32[]{:S(2)}) copy-start(bf16[128,7168]{1,0:T(8,128)(2,1)} %get-tuple-element.14) | copy-start | bytes 5505028
  101.7 9.6 %copy-start.3 = (bf16[128,512]{1,0:T(8,128)(2,1)S(1)}, bf16[128,512]{1,0:T(8,128)(2,1)}, u32[]{:S(2)}) copy-start(bf16[128,512]{1,0:T(8,128)(2,1)} %get-tuple-element.12) | copy-start | bytes 393220
  101.7 19.9 %all-to-all-start = ((bf16[32,16,256]{2,1,0:T(8,128)(2,1)}), bf16[32,16,256]{2,1,0:T(8,128)(2,1)S(1)}, u32[]{:S(2)}, u32[]{:S(2)}) async-start(bf16[32,16,256]{2,1,0:T(8,128)(2,1)} %get-tuple-element.11), calls=%async_computation | async-start | bytes 524288 | tf_op jit(solution)/shard_map/all_to_all | solution.py:395
  104.5 12.0 %copy-start.1 = (bf16[128,7168]{1,0:T(8,128)(2,1)S(1)}, bf16[128,7168]{1,0:T(8,128)(2,1)}, u32[]{:S(2)}) copy-start(bf16[128,7168]{1,0:T(8,128)(2,1)} %get-tuple-element.16) | copy-start | bytes 5505028
  104.5 12.0 %copy-start.4 = (bf16[128,512]{1,0:T(8,128)(2,1)S(1)}, bf16[128,512]{1,0:T(8,128)(2,1)}, u32[]{:S(2)}) copy-start(bf16[128,512]{1,0:T(8,128)(2,1)} %get-tuple-element.15) | copy-start | bytes 393220

commit v3 on v2

--- a/solution.py
+++ b/solution.py
@@ -34,9 +34,9 @@
 
 def core_kernel(
     chips, steps, width,
-    pieces_ref, gate_hbm, up_hbm, down_hbm,
+    tokens_ref, cotangent_ref, slot_ref, weight_ref, gate_hbm, up_hbm, down_hbm,
     hidden_hbm, dgate_hbm, dup_hbm, x_ref, d_ref, results_ref,
-    pieces_rx, weights, pair_tx, pair_rx, local, p_tx, p_rx, s_tx, s_rx, act, out_acc, dexp_acc,
+    pieces_ref, pieces_rx, weights, pair_tx, pair_rx, local, p_tx, p_rx, s_tx, s_rx, act, out_acc, dexp_acc,
     load_sem, piece_recv, pair_recv, p_recv, s_recv, act_recv, send_sem, store_sem,
 ):
     expert = lax.axis_index("expert")
@@ -93,6 +93,38 @@
 
     out_acc[...] = jnp.zeros_like(out_acc)
     dexp_acc[...] = jnp.zeros_like(dexp_acc)
+    tile_rows, half = pieces_ref.shape[1:]
+    block = 2 * CAP
+    halves = tile_rows // block
+    line = lax.broadcasted_iota(
+        jnp.int32, (tokens_ref.shape[0], devices // shards * block), 1
+    )
+    wanted = line // block * CAP + line % CAP
+    is_token = line % block < CAP
+    by_token = jnp.zeros(line.shape, F32)
+    by_cotangent = jnp.zeros(line.shape, F32)
+    for k in range(slot_ref.shape[1]):
+        match = (slot_ref[:, k : k + 1] == wanted).astype(F32)
+        by_token += jnp.where(is_token, match, 0.0)
+        by_cotangent += jnp.where(is_token, 0.0, match * weight_ref[:, k : k + 1])
+
+    def slot_rows(factors, values):
+        return lax.dot_general(
+            factors, values.astype(F32), (((0,), (0,)), ((), ())),
+            precision=lax.Precision.HIGHEST, preferred_element_type=F32,
+        )
+
+    for s in range(shards):
+        for h in range(halves):
+            begin = (s * halves + h) * half
+            span = slice(begin, begin + half)
+            mixed_rows = slot_rows(by_token, tokens_ref[:, span]) + slot_rows(
+                by_cotangent, cotangent_ref[:, span]
+            )
+            for e in range(devices // shards):
+                pieces_ref[e * shards + s, h * block : (h + 1) * block, :] = mixed_rows[
+                    e * block : (e + 1) * block
+                ].astype(BF16)
     pieces_rx[me] = pieces_ref[me]
     pl.semaphore_wait(barrier, devices - 1)
 
@@ -120,10 +152,8 @@
 
     lax.fori_loop(1, devices, send_piece, 0)
     lax.fori_loop(1, devices, await_piece, 0)
-    tile_rows, half = pieces_ref.shape[1:]
     rows = devices * CAP
     mixed = pieces_rx[...].reshape(devices * tile_rows, half)
-    halves = tile_rows // (2 * CAP)
 
     def picks(kind, h, transposed):
         shape = (devices * tile_rows, rows) if transposed else (rows, devices * tile_rows)
@@ -284,11 +314,13 @@
     return None
 
 
-def expert_core(pieces, w_gate, w_up, w_down, width):
+def expert_core(tokens, cotangent, slot_index, route_weight, w_gate, w_up, w_down, width):
     shards = lax.axis_size("shard")
-    devices = pieces.shape[0]
+    devices = lax.axis_size("expert") * shards
     rows = devices * CAP
     part, units = w_gate.shape
+    halves = 16 // (2 * CAP)
+    pieces = jax.ShapeDtypeStruct((devices, 16, part // halves), BF16)
     steps = units // 2 // width
     chips = shards // 2
     anywhere = pl.BlockSpec(memory_space=pl.ANY)
@@ -299,10 +331,11 @@
         functools.partial(core_kernel, chips, steps, width),
         out_shape=[jax.ShapeDtypeStruct((rows, units), BF16)] * 3
         + [jax.ShapeDtypeStruct((rows, part), BF16)] * 2
-        + [jax.ShapeDtypeStruct(pieces.shape, BF16)],
-        in_specs=[vmem] + [anywhere] * 3,
+        + [pieces],
+        in_specs=[vmem] * 4 + [anywhere] * 3,
         out_specs=[anywhere] * 3 + [vmem] * 3,
         scratch_shapes=[
+            pltpu.VMEM(pieces.shape, BF16),
             pltpu.VMEM(pieces.shape, BF16),
             pltpu.VMEM((2 * steps, 3, part, width), BF16),
             pltpu.VMEM(block, BF16),
@@ -328,7 +361,7 @@
             collective_id=0, has_side_effects=True, vmem_limit_bytes=VMEM_BYTES
         ),
         name="expert_core",
-    )(pieces, w_gate, w_up, w_down)
+    )(tokens, cotangent, slot_index, route_weight, w_gate, w_up, w_down)
 
 
 def expert_plain(x_rows, d_rows, w_gate, w_up, w_down):
@@ -360,29 +393,29 @@
     slot_match = (slot_index[:, :, None] == columns[None, None, :]).astype(jnp.float32)
     dispatch = jnp.sum(slot_match, axis=1).astype(jnp.bfloat16)
     combine = jnp.sum(slot_match * route_weight[:, :, None], axis=1)
-    x_slots = jnp.einsum("tc,td->cd", dispatch, tokens, preferred_element_type=jnp.float32).astype(
-        jnp.bfloat16
-    )
-    d_slots = jnp.dot(
-        combine.T, cotangent.astype(jnp.float32), precision=lax.Precision.HIGHEST
-    ).astype(jnp.bfloat16)
-
     hidden_units = w_gate.shape[2]
     devices = experts * shards
     width_step = plan(shards, rows, part, hidden_units)
     halves = 16 // (2 * CAP) if width_step else 1
 
-    both = jnp.stack([x_slots, d_slots]).reshape(
-        2, experts, CAP, shards, halves, part // halves
-    )
-    pieces = both.transpose(1, 3, 4, 0, 2, 5).reshape(
-        devices, halves * 2 * CAP, part // halves
-    )
     if width_step:
         hidden, d_gate, d_up, x_rows, d_rows, results = expert_core(
-            pieces, w_gate[0], w_up[0], w_down[0], width_step
+            tokens, cotangent, slot_index, route_weight,
+            w_gate[0], w_up[0], w_down[0], width_step,
         )
     else:
+        x_slots = jnp.einsum("tc,td->cd", dispatch, tokens, preferred_element_type=jnp.float32).astype(
+            jnp.bfloat16
+        )
+        d_slots = jnp.dot(
+            combine.T, cotangent.astype(jnp.float32), precision=lax.Precision.HIGHEST
+        ).astype(jnp.bfloat16)
+        both = jnp.stack([x_slots, d_slots]).reshape(
+            2, experts, CAP, shards, halves, part // halves
+        )
+        pieces = both.transpose(1, 3, 4, 0, 2, 5).reshape(
+            devices, halves * 2 * CAP, part // halves
+        )
         arrived = lax.all_to_all(pieces, BOTH, split_axis=0, concat_axis=0, tiled=True)
         x_rows = arrived[:, :CAP].reshape(rows, part)
         d_rows = arrived[:, CAP:].reshape(rows, part)

time: 124 us -> 124 us (level)
  local copies, waits for them, and re-layouts: 1.72 us -> 3.59 us
  matrix products: 20.1 us -> 18.7 us
    unnamed x10 -> x15, local copies, waits for them, and re-layouts: 0.03 us -> 2.88 us
    dot_general x2 -> x0, matrix products: 1.38 us -> none  [the longest x1 1.16 us: per_device(): jnp.dot(combine.T, cotangent.astype(jnp.float32), precision=lax.Precision...]
where the time goes in v3:
time: 124 us; the launch traced here: 123 us
  Pallas kernels  96.8 us (78%)
  matrix products  18.7 us (15%)
  local copies, waits for them, and re-layouts  3.59 us (3%)
  starting transfers between devices  2.73 us (2%)
    pallas_call x1, Pallas kernels, expert_core(): pl.pallas_call(functools.partial(core_kernel, chips, steps, width), out_s...  96.8 us
    dot_general x3, matrix products, grad(): jnp.einsum('rd,rf->df', left, right, preferred_element_type=jnp.float32)  17.1 us
    unnamed x15, local copies, waits for them, and re-layouts  2.88 us
    all_to_all x1, starting transfers between devices, per_device(): lax.all_to_all(results, BOTH, split_axis=0, concat_axis=0, tiled=True)  2.73 us
  transfers between devices with their start and end apart: 1, of which 0 were waited for; matrix products, arithmetic and copies ran while one was open for 14% of the time, Pallas kernels for 0%

profile of v3, /device:TPU:0, one launch (start us, length us, event | category | flops | bytes accessed | tf_op | source)
XLA Modules:
  0.0 123.3 jit_solution(16463402967353334651)
XLA Ops:
  0.6 0.8 copy.22
  1.4 0.8 copy.23
  2.1 1.3 %copy.25.weight_ref = f32[8,2]{1,0:T(8,128)} copy(f32[8,2]{0,1:T(2,128)} %param.12) | data formatting | bytes 128 | tf_op args[4]
  3.5 0.6 multiply_add_fusion.slot_ref
  4.1 0.0 copy-start.4
  4.1 96.8 %expert_core.1 = (bf16[128,7168]{1,0:T(8,128)(2,1)}, bf16[128,7168]{1,0:T(8,128)(2,1)}, bf16[128,7168]{1,0:T(8,128)(2,1)}, bf16[128,512]{1,0:T(8,128)(2,1)}, bf1...) custom-call(bf16[8,4096]{1,0:T(8,128)(2,1)} %tokens_ref.1, bf16[8,4096]{1,0:T(8,128)(2,1)} %cotangent_ref.1, ...), custom_call_target="tpu_custom_call" | custom-call | tf_op jit(solution)/shard_map/expert_core/pallas_call | solution.py:330
  100.9 0.0 copy-start.5
  100.9 0.0 copy-start.1
  101.0 0.0 copy-start.2
  101.0 2.7 %all-to-all-start = ((bf16[32,16,256]{2,1,0:T(8,128)(2,1)}), bf16[32,16,256]{2,1,0:T(8,128)(2,1)S(1)}, u32[]{:S(2)}, u32[]{:S(2)}) async-start(bf16[32,16,256]{2,1,0:T(8,128)(2,1)} %get-tuple-element.11), calls=%async_computation | async-start | bytes 524288 | tf_op jit(solution)/shard_map/all_to_all | solution.py:428
  103.7 0.0 copy-done.4
  103.7 0.1 copy.24
  103.8 0.0 copy-start
  103.8 0.0 copy-start.3
  103.8 6.8 %fusion = bf16[1,512,7168]{2,1,0:T(8,128)(2,1)} fusion(bf16[128,512]{1,0:T(8,128)(2,1)} %get-tuple-element.12, bf16[128,7168]{1,0:T(8,128)(2,1)} %get-tuple-element.13), kind=kOutput, calls=%fused_computation.3 | convolution fusion | flops 943194112 | bytes 9306112 | tf_op jit(solution)/shard_map/rd,rf->df/dot_general | solution.py:439
  110.6 0.0 copy-done.5
  110.6 0.1 convert_reduce_fusion
  110.7 0.0 copy-done.1
  110.7 0.0 copy-done.2
  110.7 5.1 %fusion.1 = bf16[1,512,7168]{2,1,0:T(8,128)(2,1)} fusion(bf16[128,512]{1,0:T(8,128)(2,1)S(1)} %copy-done.2, bf16[128,7168]{1,0:T(8,128)(2,1)S(1)} %copy-done.1), kind=kOutput, calls=%fused_computation.4 | convolution fusion | flops 943194112 | bytes 9306112 | tf_op jit(solution)/shard_map/rd,rf->df/dot_general | solution.py:439
  115.9 0.0 copy-done
  115.9 0.0 copy-done.3
  115.9 5.1 %fusion.2 = bf16[1,512,7168]{2,1,0:T(8,128)(2,1)} fusion(bf16[128,512]{1,0:T(8,128)(2,1)S(1)} %copy-done.3, bf16[128,7168]{1,0:T(8,128)(2,1)S(1)} %copy-done), kind=kOutput, calls=%fused_computation.5 | convolution fusion | flops 943194112 | bytes 9306112 | tf_op jit(solution)/shard_map/rd,rf->df/dot_general | solution.py:439
  121.0 0.0 all-to-all-done
  121.0 0.1 reshape.20
  121.1 0.2 copy.28
  121.3 0.2 fusion.4
  121.5 0.1 squeeze.19
  121.6 0.1 squeeze.18
  121.7 0.8 convolution_convert_fusion.3
  122.5 0.8 convolution_convert_fusion.4
Async XLA Ops:
  4.1 99.6 %copy-start.4 = (s32[8,2]{1,0:T(8,128)S(1)}, s32[8,2]{1,0:T(8,128)}, u32[]{:S(2)}) copy-start(s32[8,2]{1,0:T(8,128)} %multiply_add_fusion.slot_ref) | copy-start | bytes 196
  100.9 9.7 %copy-start.5 = (f32[8,2]{0,1:T(2,128)S(1)}, f32[8,2]{0,1:T(2,128)}, u32[]{:S(2)}) copy-start(f32[8,2]{0,1:T(2,128)} %param.12) | copy-start | bytes 196
  100.9 9.8 %copy-start.1 = (bf16[128,7168]{1,0:T(8,128)(2,1)S(1)}, bf16[128,7168]{1,0:T(8,128)(2,1)}, u32[]{:S(2)}) copy-start(bf16[128,7168]{1,0:T(8,128)(2,1)} %get-tuple-element.14) | copy-start | bytes 5505028
  101.0 9.8 %copy-start.2 = (bf16[128,512]{1,0:T(8,128)(2,1)S(1)}, bf16[128,512]{1,0:T(8,128)(2,1)}, u32[]{:S(2)}) copy-start(bf16[128,512]{1,0:T(8,128)(2,1)} %get-tuple-element.12) | copy-start | bytes 393220
  101.0 20.1 %all-to-all-start = ((bf16[32,16,256]{2,1,0:T(8,128)(2,1)}), bf16[32,16,256]{2,1,0:T(8,128)(2,1)S(1)}, u32[]{:S(2)}, u32[]{:S(2)}) async-start(bf16[32,16,256]{2,1,0:T(8,128)(2,1)} %get-tuple-element.11), calls=%async_computation | async-start | bytes 524288 | tf_op jit(solution)/shard_map/all_to_all | solution.py:428
  103.8 12.1 %copy-start = (bf16[128,7168]{1,0:T(8,128)(2,1)S(1)}, bf16[128,7168]{1,0:T(8,128)(2,1)}, u32[]{:S(2)}) copy-start(bf16[128,7168]{1,0:T(8,128)(2,1)} %get-tuple-element.16) | copy-start | bytes 5505028
  103.8 12.1 %copy-start.3 = (bf16[128,512]{1,0:T(8,128)(2,1)S(1)}, bf16[128,512]{1,0:T(8,128)(2,1)}, u32[]{:S(2)}) copy-start(bf16[128,512]{1,0:T(8,128)(2,1)} %get-tuple-element.15) | copy-start | bytes 393220
